TPU v7x, 256 devices: a whole 4x4x8 slice. The times are simulated.
256 devices in a mesh: grp: 16 (over z_lo, y, core), dp: 16 (over x, z_hi).
Axes of the slice: x: 4, y: 4, z: 8 (z_hi: 4, z_lo: 2; z = z_hi * 2 + z_lo), core: 2. Of those that a mesh axis runs over, the one named last changes fastest.
Arguments:
- queries: bfloat16 [16, 16, 128, 2048], P('dp', 'grp'), may hold values from -18 to 18
- mem_keys: bfloat16 [16, 16, 256, 2048], P('dp', 'grp'), may hold values from -18 to 18
- mem_values: bfloat16 [16, 16, 256, 2048], P('dp', 'grp'), may hold values from -48 to 48
- lengths: int32 [16, 16], P('dp'), may hold values from 128 to 256, as said below
- mates: int32 [16, 16, 16], P('dp'), may hold values 0 or 1
- out_grad: bfloat16 [16, 16, 128, 2048], P('dp', 'grp'), may hold values from -6 to 6
- mlp_input: bfloat16 [16, 16, 128, 4096], P('dp', 'grp'), may hold values from -6 to 6
- gate_pre: bfloat16 [16, 16, 128, 5632], P('dp', 'grp'), may hold values from -6 to 6
- hidden_grad: bfloat16 [16, 16, 128, 5632], P('dp', 'grp'), may hold values from -0.03125 to 0.03125
Outputs:
- attn_out: bfloat16 [16, 16, 128, 2048], P('dp', 'grp')
- q_grad: bfloat16 [16, 16, 128, 2048], P('dp', 'grp')
- up_grad: float32 [4096, 5632], P(None, ('grp', 'dp'))
Inputs may be any that keep to these rules, and one draw needn't show every extreme that they name: `lengths`: each is a multiple of 128; in every group some document has 256. `mates`: A document reads its own previous context whatever its diagonal entry.
All inputs are finite; a program needn't handle non-finite values. No bound on the sum of `mates` on one device may be relied on, other than what follows from the above.
Results may differ from a plain program's by a relative error of at most 0.025.
Values may be sent and summed in bfloat16 or wider, within the bound.
No kernel may reach another device: no remote copies, remote signals or barrier semaphores. Data moves between devices by JAX's collectives and lax.ppermute only.
A program may use at most 128 MiB of HBM per device.

v0:
```python
import math
import jax
import jax.numpy as jnp
from jax import lax
from jax.sharding import Mesh
from jax.sharding import PartitionSpec as P

HEAD_DIM = 128
DP = ("dp_0", "dp_1")
GRP_DP = ("grp", "dp_0", "dp_1")


def summed_rows(x, axes, dim):
    if not axes:
        return x
    nearer = lax.psum_scatter(x, axes[0], scatter_dimension=dim, tiled=True)
    return summed_rows(nearer, axes[1:], dim)


def head_pass(query_head, key_head, value_head, grad_head, key_mask):
    inv_root = 1.0 / math.sqrt(query_head.shape[1])
    scores = jnp.dot(query_head, key_head.T, preferred_element_type=jnp.float32) * inv_root
    scores = jnp.where(key_mask, scores, -1e30)
    highest = jnp.max(scores, axis=1, keepdims=True)
    weights = jnp.exp(scores - highest)
    row_total = jnp.sum(weights, axis=1, keepdims=True)
    weights_bf = (weights / row_total).astype(jnp.bfloat16)
    result = jnp.dot(weights_bf, value_head, preferred_element_type=jnp.float32).astype(
        jnp.bfloat16
    )
    grad_weights = jnp.dot(grad_head, value_head.T, preferred_element_type=jnp.float32)
    row_dot = jnp.sum(
        grad_head.astype(jnp.float32) * result.astype(jnp.float32), axis=1, keepdims=True
    )
    grad_scores = (weights_bf.astype(jnp.float32) * (grad_weights - row_dot)).astype(jnp.bfloat16)
    grad_query = (
        jnp.dot(grad_scores, key_head, preferred_element_type=jnp.float32) * inv_root
    ).astype(jnp.bfloat16)
    return (result, grad_query)


def per_device(
    queries, mem_keys, mem_values, lengths, mates, out_grad, mlp_input, gate_pre, hidden_grad
):
    members = lax.axis_size("grp")
    rows_q = queries.shape[2]
    mem_rows = mem_keys.shape[2]
    heads_all = queries.shape[3] // HEAD_DIM
    local_heads = heads_all // members
    docs_block = max(1, min(members, 512 // rows_q))
    block_count = members // docs_block
    row_count = docs_block * rows_q
    allowed = (mates[0] > 0) | jnp.eye(members, dtype=bool)
    live_keys = jnp.arange(mem_rows, dtype=jnp.int32)[None, :] < lengths[0][:, None]

    def split_heads(block):
        return block[0, 0].reshape(block.shape[2], members, local_heads, HEAD_DIM)

    def per_head(pieces):
        query_head, key_head, value_head, grad_head = pieces

        def block_step(block_num):
            first_row = block_num * row_count
            query_rows = lax.dynamic_slice_in_dim(query_head, first_row, row_count, 0)
            grad_rows = lax.dynamic_slice_in_dim(grad_head, first_row, row_count, 0)
            allowed_rows = lax.dynamic_slice_in_dim(allowed, block_num * docs_block, docs_block, 0)
            key_mask = jnp.broadcast_to(
                allowed_rows[:, None, :, None] & live_keys[None, None, :, :],
                (docs_block, rows_q, members, mem_rows),
            )
            key_mask = key_mask.reshape(row_count, members * mem_rows)
            return head_pass(query_rows, key_head, value_head, grad_rows, key_mask)

        results, gradients = lax.map(block_step, jnp.arange(block_count))
        return (
            results.reshape(members * rows_q, HEAD_DIM),
            gradients.reshape(members * rows_q, HEAD_DIM),
        )

    exchanged = (
        lax.all_to_all(split_heads(queries), "grp", split_axis=1, concat_axis=0, tiled=True),
        lax.all_to_all(split_heads(mem_keys), "grp", split_axis=1, concat_axis=0, tiled=True),
        lax.all_to_all(split_heads(mem_values), "grp", split_axis=1, concat_axis=0, tiled=True),
        lax.all_to_all(split_heads(out_grad), "grp", split_axis=1, concat_axis=0, tiled=True),
    )
    query_all, key_all, value_all, grad_all = [
        jnp.moveaxis(member[:, 0], 1, 0) for member in exchanged
    ]
    results, gradients = lax.map(per_head, (query_all, key_all, value_all, grad_all))
    heads_out = jnp.moveaxis(results, 0, 1)[:, None]
    heads_grad = jnp.moveaxis(gradients, 0, 1)[:, None]
    back_out, back_grad = (
        lax.all_to_all(heads_out, "grp", split_axis=0, concat_axis=1, tiled=True),
        lax.all_to_all(heads_grad, "grp", split_axis=0, concat_axis=1, tiled=True),
    )
    attn_out = back_out.reshape(1, 1, rows_q, heads_all * HEAD_DIM)
    q_grad = back_grad.reshape(1, 1, rows_q, heads_all * HEAD_DIM)
    up_cot = (
        hidden_grad[0, 0].astype(jnp.float32) * jax.nn.silu(gate_pre[0, 0].astype(jnp.float32))
    ).astype(jnp.bfloat16)
    tokens = mlp_input[0, 0]
    contract = (((0,), (0,)), ((), ()))
    slices = lax.all_to_all(up_cot, "grp", split_axis=1, concat_axis=0, tiled=True)
    partial_value = lax.dot_general(
        lax.all_gather(tokens, "grp", axis=0, tiled=True),
        slices,
        contract,
        preferred_element_type=jnp.float32,
    )
    up_grad = summed_rows(partial_value.astype(jnp.bfloat16), DP, 1).astype(jnp.float32)
    return (attn_out, q_grad, up_grad)


def solution(mesh):
    finer = Mesh(mesh.devices.reshape(mesh.shape["grp"], 4, 4), ("grp", "dp_0", "dp_1"))
    return jax.shard_map(
        per_device,
        mesh=finer,
        in_specs=(
            P(DP, "grp", None, None),
            P(DP, "grp", None, None),
            P(DP, "grp", None, None),
            P(DP, None),
            P(DP, None, None),
            P(DP, "grp", None, None),
            P(DP, "grp", None, None),
            P(DP, "grp", None, None),
            P(DP, "grp", None, None),
        ),
        out_specs=(P(DP, "grp", None, None), P(DP, "grp", None, None), P(None, GRP_DP)),
        check_vma=False,
    )
```

profile of v0, /device:TPU:72, one launch (start us, length us, event | category | flops | bytes accessed | tf_op | source)
XLA Modules:
  0.0 324.0 jit_solution(11458148541503357170)
XLA Ops:
  9.9 6.3 %all-to-all-start.3 = ((bf16[128,16,1,128]{0,3,2,1:T(8,128)(2,1)}), bf16[128,16,1,128]{0,3,2,1:T(8,128)(2,1)S(1)}, u32[]{:S(2)}, u32[]{:S(2)}) async-start(bf16[128,16,1,128]{0,3,2,1:T(8,128)(2,1)} %bitcast.13), calls=%async_computation.3 | async-start | bytes 1048576 | tf_op jit(solution)/shard_map/all_to_all | solution.py:84
  18.6 4.9 %all-to-all-done.3 = bf16[128,16,1,128]{0,3,2,1:T(8,128)(2,1)S(1)} async-done(((bf16[128,16,1,128]{0,3,2,1:T(8,128)(2,1)}), bf16[128,16,1,128]{0,3,2,1:T(8,128)(2,1)S(1)}, u32[]{:S(2)}, u32[]{:S(2)}) %all-to-all-start.3) | async-done | bytes 524320 | tf_op jit(solution)/shard_map/all_to_all | solution.py:84
  23.4 7.1 %all-to-all-start = ((bf16[128,16,1,128]{3,0,2,1:T(8,128)(2,1)}), bf16[128,16,1,128]{3,0,2,1:T(8,128)(2,1)S(1)}, u32[]{:S(2)}, u32[]{:S(2)}) async-start(bf16[128,16,1,128]{3,0,2,1:T(8,128)(2,1)} %copy.51), calls=%async_computation | async-start | bytes 1048576 | tf_op jit(solution)/shard_map/all_to_all | solution.py:81
  32.4 9.4 %all-to-all-done = bf16[128,16,1,128]{3,0,2,1:T(8,128)(2,1)S(1)} async-done(((bf16[128,16,1,128]{3,0,2,1:T(8,128)(2,1)}), bf16[128,16,1,128]{3,0,2,1:T(8,128)(2,1)S(1)}, u32[]{:S(2)}, u32[]{:S(2)}) %all-to-all-start) | async-done | bytes 524320 | tf_op jit(solution)/shard_map/all_to_all | solution.py:81
  41.8 9.3 %all-to-all-start.2 = ((bf16[256,16,1,128]{3,0,2,1:T(8,128)(2,1)}), bf16[256,16,1,128]{3,0,2,1:T(8,128)(2,1)S(1)}, u32[]{:S(2)}, u32[]{:S(2)}) async-start(bf16[256,16,1,128]{3,0,2,1:T(8,128)(2,1)} %copy.55), calls=%async_computation.2 | async-start | bytes 2097152 | tf_op jit(solution)/shard_map/all_to_all | solution.py:83
  55.4 3.4 %fusion.23 = bf16[128,16,352]{0,2,1:T(8,128)(2,1)} fusion(bf16[128,16,352]{0,2,1:T(8,128)(2,1)S(1)} %bitcast.105, bf16[128,16,352]{0,2,1:T(8,128)(2,1)} %bitcast.106), kind=kLoop, calls=%fused_computation.30 | loop fusion | flops 5767168 | bytes 4325376 | tf_op jit(solution)/shard_map/convert_element_type | solution.py:100
  58.8 11.8 %all-to-all-done.2 = bf16[256,16,1,128]{3,0,2,1:T(8,128)(2,1)S(1)} async-done(((bf16[256,16,1,128]{3,0,2,1:T(8,128)(2,1)}), bf16[256,16,1,128]{3,0,2,1:T(8,128)(2,1)S(1)}, u32[]{:S(2)}, u32[]{:S(2)}) %all-to-all-start.2) | async-done | bytes 1048608 | tf_op jit(solution)/shard_map/all_to_all | solution.py:83
  70.6 12.9 %all-to-all-start.6 = ((bf16[128,16,352]{0,2,1:T(8,128)(2,1)}), bf16[128,16,352]{0,2,1:T(8,128)(2,1)}, u32[]{:S(2)}, u32[]{:S(2)}) async-start(bf16[128,16,352]{0,2,1:T(8,128)(2,1)} %fusion.23), calls=%async_computation.6 | async-start | bytes 2883584 | tf_op jit(solution)/shard_map/all_to_all | solution.py:103
  86.3 23.1 %all-to-all-done.6 = bf16[128,16,352]{0,2,1:T(8,128)(2,1)} async-done(((bf16[128,16,352]{0,2,1:T(8,128)(2,1)}), bf16[128,16,352]{0,2,1:T(8,128)(2,1)}, u32[]{:S(2)}, u32[]{:S(2)}) %all-to-all-start.6) | async-done | bytes 1441824 | tf_op jit(solution)/shard_map/all_to_all | solution.py:103
  109.4 14.3 %all-to-all-start.1 = ((bf16[256,16,1,128]{3,0,2,1:T(8,128)(2,1)}), bf16[256,16,1,128]{3,0,2,1:T(8,128)(2,1)S(1)}, u32[]{:S(2)}, u32[]{:S(2)}) async-start(bf16[256,16,1,128]{3,0,2,1:T(8,128)(2,1)} %copy.53), calls=%async_computation.1 | async-start | bytes 2097152 | tf_op jit(solution)/shard_map/all_to_all | solution.py:82
  124.9 24.6 %all-gather.3.cloned.1.call-done = bf16[1,1,2048,4096]{3,2,1,0:T(8,128)(2,1)} async-done(((bf16[1,1,128,4096]{3,2,1,0:T(8,128)(2,1)}), bf16[1,1,2048,4096]{3,2,1,0:T(8,128)(2,1)}) %all-gather.3.cloned.1.call-update) | async-done | bytes 16777232 | tf_op jit(solution)/shard_map/all_gather | solution.py:105
  149.5 13.4 %fusion.16 = bf16[4096,352]{0,1:T(8,128)(2,1)} fusion(bf16[1,1,2048,4096]{3,2,1,0:T(8,128)(2,1)} %all-gather.3.cloned.1.call-done, bf16[128,16,352]{0,2,1:T(8,128)(2,1)} %all-to-all-done.6), kind=kOutput, calls=%fused_computation.23 | convolution fusion | flops 5907021824 | bytes 21102592 | tf_op jit(solution)/shard_map/dot_general | solution.py:104
  163.0 92.8 %while.22 = (s32[]{:T(128)}, bf16[4,512,128]{2,1,0:T(8,128)(2,1)}, bf16[4,512,128]{2,1,0:T(8,128)(2,1)}, s32[4]{0:T(128)S(1)}, pred[16,16]{1,0:T(8,128)(4,1)S(1)...) while((s32[]{:T(128)}, bf16[4,512,128]{2,1,0:T(8,128)(2,1)}, ...), condition=%wide.region_4.5_spmd.clone, body=%wide.region_0.4_spmd.clone.sunk | while | flops 2173127168 | bytes 64675448 | solution.py:74
  167.5 3.2 %fusion.50 = (f32[512]{0:T(512)S(1)}, f32[512,4096]{1,0:T(8,128)S(1)}) fusion(pred[512,4096]{1,0:T(8,128)(4,1)S(1)} %bitcast.102, bf16[4096,128]{1,0:T(8,128)(2,1)} %copy-done.1, bf16[2048,128]{1,0:T(8,128)(2,1)} %copy-done.3, s32[]{:T(128)S(6)} %select_n.17), kind=kOutput, calls=%fused_computation.36.clone.1 | convolution fusion | flops 543161856 | bytes 11667460 | tf_op jit(solution)/shard_map/while/body/eval_jaxpr/while/body/eval_jaxpr/dot_general | solution.py:22
  172.0 3.3 %divide_convert_fusion.2 = bf16[512,4096]{1,0:T(8,128)(2,1)} fusion(f32[512,4096]{1,0:T(8,128)S(1)} %get-tuple-element.256, f32[512]{0:T(512)S(1)} %fusion.51, f32[512]{0:T(512)S(1)} %get-tuple-element.257), kind=kLoop, calls=%fused_computation.2.clone.1 | loop fusion | flops 6291456 | bytes 12587008 | tf_op jit(solution)/shard_map/while/body/eval_jaxpr/while/body/eval_jaxpr/convert_element_type | solution.py:27
  176.5 3.7 %multiply_reduce_fusion.2 = (f32[512]{0:T(512)S(1)}, bf16[512,128]{0,1:T(8,128)(2,1)S(1)}) fusion(bf16[512,128]{0,1:T(8,128)(2,1)S(1)} %copy.86, bf16[512,4096]{1,0:T(8,128)(2,1)} %divide_convert_fusion.2, bf16[4096,128]{1,0:T(8,128)(2,1)S(1)} %get-tuple-element.299), kind=kOutput, calls=%fused_computation.12.clone.1 | convolution fusion | flops 537198080 | bytes 5507072 | tf_op jit(solution)/shard_map/while/body/eval_jaxpr/while/body/eval_jaxpr/dot_general | solution.py:28
  180.2 5.4 %fusion.52 = bf16[4,512,128]{2,1,0:T(8,128)(2,1)} fusion(bf16[4,512,128]{2,1,0:T(8,128)(2,1)} %get-tuple-element.278, s32[]{:T(128)} %get-tuple-element.276, bf16[4096,128]{1,0:T(8,128)(2,1)S(1)} %copy-done.2, bf16[512,4096]{1,0:T(8,128)(2,1)} %divide_convert_fusion.2, bf16[512,128]{1,0:T(8,128)(2,1)S(1)} %constant_dynamic-slice_fusion.4, ...), kind=kOutput, calls=%fused_computation.11.clone.1 | convolution fusion | flops 1082261504 | bytes 6556160 | tf_op jit(solution)/shard_map/while/body/eval_jaxpr/while/body/eval_jaxpr/dot_general | solution.py:37
  195.2 3.3 %divide_convert_fusion.2 = bf16[512,4096]{1,0:T(8,128)(2,1)} fusion(f32[512,4096]{1,0:T(8,128)S(1)} %get-tuple-element.256, f32[512]{0:T(512)S(1)} %fusion.51, f32[512]{0:T(512)S(1)} %get-tuple-element.257), kind=kLoop, calls=%fused_computation.2.clone.1 | loop fusion | flops 6291456 | bytes 12587008 | tf_op jit(solution)/shard_map/while/body/eval_jaxpr/while/body/eval_jaxpr/convert_element_type | solution.py:27
  199.6 3.7 %multiply_reduce_fusion.2 = (f32[512]{0:T(512)S(1)}, bf16[512,128]{0,1:T(8,128)(2,1)S(1)}) fusion(bf16[512,128]{0,1:T(8,128)(2,1)S(1)} %copy.86, bf16[512,4096]{1,0:T(8,128)(2,1)} %divide_convert_fusion.2, bf16[4096,128]{1,0:T(8,128)(2,1)S(1)} %get-tuple-element.299), kind=kOutput, calls=%fused_computation.12.clone.1 | convolution fusion | flops 537198080 | bytes 5507072 | tf_op jit(solution)/shard_map/while/body/eval_jaxpr/while/body/eval_jaxpr/dot_general | solution.py:28
  203.4 5.4 %fusion.52 = bf16[4,512,128]{2,1,0:T(8,128)(2,1)} fusion(bf16[4,512,128]{2,1,0:T(8,128)(2,1)} %get-tuple-element.278, s32[]{:T(128)} %get-tuple-element.276, bf16[4096,128]{1,0:T(8,128)(2,1)S(1)} %copy-done.2, bf16[512,4096]{1,0:T(8,128)(2,1)} %divide_convert_fusion.2, bf16[512,128]{1,0:T(8,128)(2,1)S(1)} %constant_dynamic-slice_fusion.4, ...), kind=kOutput, calls=%fused_computation.11.clone.1 | convolution fusion | flops 1082261504 | bytes 6556160 | tf_op jit(solution)/shard_map/while/body/eval_jaxpr/while/body/eval_jaxpr/dot_general | solution.py:37
  213.8 3.2 %fusion.50 = (f32[512]{0:T(512)S(1)}, f32[512,4096]{1,0:T(8,128)S(1)}) fusion(pred[512,4096]{1,0:T(8,128)(4,1)S(1)} %bitcast.102, bf16[4096,128]{1,0:T(8,128)(2,1)} %copy-done.1, bf16[2048,128]{1,0:T(8,128)(2,1)} %copy-done.3, s32[]{:T(128)S(6)} %select_n.17), kind=kOutput, calls=%fused_computation.36.clone.1 | convolution fusion | flops 543161856 | bytes 11667460 | tf_op jit(solution)/shard_map/while/body/eval_jaxpr/while/body/eval_jaxpr/dot_general | solution.py:22
  218.3 3.3 %divide_convert_fusion.2 = bf16[512,4096]{1,0:T(8,128)(2,1)} fusion(f32[512,4096]{1,0:T(8,128)S(1)} %get-tuple-element.256, f32[512]{0:T(512)S(1)} %fusion.51, f32[512]{0:T(512)S(1)} %get-tuple-element.257), kind=kLoop, calls=%fused_computation.2.clone.1 | loop fusion | flops 6291456 | bytes 12587008 | tf_op jit(solution)/shard_map/while/body/eval_jaxpr/while/body/eval_jaxpr/convert_element_type | solution.py:27
  222.8 3.7 %multiply_reduce_fusion.2 = (f32[512]{0:T(512)S(1)}, bf16[512,128]{0,1:T(8,128)(2,1)S(1)}) fusion(bf16[512,128]{0,1:T(8,128)(2,1)S(1)} %copy.86, bf16[512,4096]{1,0:T(8,128)(2,1)} %divide_convert_fusion.2, bf16[4096,128]{1,0:T(8,128)(2,1)S(1)} %get-tuple-element.299), kind=kOutput, calls=%fused_computation.12.clone.1 | convolution fusion | flops 537198080 | bytes 5507072 | tf_op jit(solution)/shard_map/while/body/eval_jaxpr/while/body/eval_jaxpr/dot_general | solution.py:28
  226.5 5.4 %fusion.52 = bf16[4,512,128]{2,1,0:T(8,128)(2,1)} fusion(bf16[4,512,128]{2,1,0:T(8,128)(2,1)} %get-tuple-element.278, s32[]{:T(128)} %get-tuple-element.276, bf16[4096,128]{1,0:T(8,128)(2,1)S(1)} %copy-done.2, bf16[512,4096]{1,0:T(8,128)(2,1)} %divide_convert_fusion.2, bf16[512,128]{1,0:T(8,128)(2,1)S(1)} %constant_dynamic-slice_fusion.4, ...), kind=kOutput, calls=%fused_computation.11.clone.1 | convolution fusion | flops 1082261504 | bytes 6556160 | tf_op jit(solution)/shard_map/while/body/eval_jaxpr/while/body/eval_jaxpr/dot_general | solution.py:37
  241.5 3.3 %divide_convert_fusion.2 = bf16[512,4096]{1,0:T(8,128)(2,1)} fusion(f32[512,4096]{1,0:T(8,128)S(1)} %get-tuple-element.256, f32[512]{0:T(512)S(1)} %fusion.51, f32[512]{0:T(512)S(1)} %get-tuple-element.257), kind=kLoop, calls=%fused_computation.2.clone.1 | loop fusion | flops 6291456 | bytes 12587008 | tf_op jit(solution)/shard_map/while/body/eval_jaxpr/while/body/eval_jaxpr/convert_element_type | solution.py:27
  245.9 3.7 %multiply_reduce_fusion.2 = (f32[512]{0:T(512)S(1)}, bf16[512,128]{0,1:T(8,128)(2,1)S(1)}) fusion(bf16[512,128]{0,1:T(8,128)(2,1)S(1)} %copy.86, bf16[512,4096]{1,0:T(8,128)(2,1)} %divide_convert_fusion.2, bf16[4096,128]{1,0:T(8,128)(2,1)S(1)} %get-tuple-element.299), kind=kOutput, calls=%fused_computation.12.clone.1 | convolution fusion | flops 537198080 | bytes 5507072 | tf_op jit(solution)/shard_map/while/body/eval_jaxpr/while/body/eval_jaxpr/dot_general | solution.py:28
  249.6 5.4 %fusion.52 = bf16[4,512,128]{2,1,0:T(8,128)(2,1)} fusion(bf16[4,512,128]{2,1,0:T(8,128)(2,1)} %get-tuple-element.278, s32[]{:T(128)} %get-tuple-element.276, bf16[4096,128]{1,0:T(8,128)(2,1)S(1)} %copy-done.2, bf16[512,4096]{1,0:T(8,128)(2,1)} %divide_convert_fusion.2, bf16[512,128]{1,0:T(8,128)(2,1)S(1)} %constant_dynamic-slice_fusion.4, ...), kind=kOutput, calls=%fused_computation.11.clone.1 | convolution fusion | flops 1082261504 | bytes 6556160 | tf_op jit(solution)/shard_map/while/body/eval_jaxpr/while/body/eval_jaxpr/dot_general | solution.py:37
  259.3 6.4 %all-to-all-start.4 = ((bf16[16,2,8192]{2,1,0:T(2,128)(2,1)}), bf16[16,2,8192]{2,1,0:T(2,128)(2,1)S(1)}, u32[]{:S(2)}, u32[]{:S(2)}) async-start(bf16[16,2,8192]{2,1,0:T(2,128)(2,1)} %reshape.67), calls=%async_computation.4 | async-start | bytes 1048576 | tf_op jit(solution)/shard_map/all_to_all | solution.py:93
  268.7 4.2 %all-to-all-done.4 = bf16[16,2,8192]{2,1,0:T(2,128)(2,1)S(1)} async-done(((bf16[16,2,8192]{2,1,0:T(2,128)(2,1)}), bf16[16,2,8192]{2,1,0:T(2,128)(2,1)S(1)}, u32[]{:S(2)}, u32[]{:S(2)}) %all-to-all-start.4) | async-done | bytes 524320 | tf_op jit(solution)/shard_map/all_to_all | solution.py:93
  272.9 7.1 %all-to-all-start.5 = ((bf16[16,2,8192]{2,1,0:T(2,128)(2,1)}), bf16[16,2,8192]{2,1,0:T(2,128)(2,1)S(1)}, u32[]{:S(2)}, u32[]{:S(2)}) async-start(bf16[16,2,8192]{2,1,0:T(2,128)(2,1)} %reshape.69), calls=%async_computation.5 | async-start | bytes 1048576 | tf_op jit(solution)/shard_map/all_to_all | solution.py:94
  280.0 25.5 %fusion.2 = bf16[4096,24]{0,1:T(8,128)(2,1)S(1)} fusion(bf16[4096,88]{0,1:T(8,128)(2,1)} %reduce-scatter.4.cloned.1.call-done), kind=kCustom, calls=%all-reduce-scatter | all-reduce-scatter fusion | flops 393217 | bytes 918528
  305.6 5.3 %collective-permute-start = (bf16[4096,6]{0,1:T(8,128)(2,1)S(1)}, bf16[4096,6]{0,1:T(8,128)(2,1)S(1)}, u32[]{:S(2)}, u32[]{:S(2)}) collective-permute-start(bf16[4096,6]{0,1:T(8,128)(2,1)S(1)} %slice), channel_id=1, source_target_pairs={{0,1},{1,2},{2,3},{4,5},{5,6},{6,7},{8,9},{9,10},{10,11},{12,13},{... | collective-permute-start | bytes 147464
  (125 shorter events, 58.5 us)
Async XLA Ops:
  7.2 23.4 %copy-start = (bf16[1,1,256,2048]{3,2,1,0:T(8,128)(2,1)S(1)}, bf16[1,1,256,2048]{3,2,1,0:T(8,128)(2,1)}, u32[]{:S(2)}) copy-start(bf16[1,1,256,2048]{3,2,1,0:T(8,128)(2,1)} %param.13) | copy-start | bytes 3145732
  7.2 142.3 %all-gather.3.cloned.1.call-start = ((), (), s32[]{:S(2)}) async-start(), calls=%async_computation.9 | async-start | bytes 17825792 | tf_op jit(solution)/shard_map/all_gather | solution.py:105
  9.9 13.5 %all-to-all-start.3 = ((bf16[128,16,1,128]{0,3,2,1:T(8,128)(2,1)}), bf16[128,16,1,128]{0,3,2,1:T(8,128)(2,1)S(1)}, u32[]{:S(2)}, u32[]{:S(2)}) async-start(bf16[128,16,1,128]{0,3,2,1:T(8,128)(2,1)} %bitcast.13), calls=%async_computation.3 | async-start | bytes 1048576 | tf_op jit(solution)/shard_map/all_to_all | solution.py:84
  23.4 18.3 %all-to-all-start = ((bf16[128,16,1,128]{3,0,2,1:T(8,128)(2,1)}), bf16[128,16,1,128]{3,0,2,1:T(8,128)(2,1)S(1)}, u32[]{:S(2)}, u32[]{:S(2)}) async-start(bf16[128,16,1,128]{3,0,2,1:T(8,128)(2,1)} %copy.51), calls=%async_computation | async-start | bytes 1048576 | tf_op jit(solution)/shard_map/all_to_all | solution.py:81
  41.8 28.8 %all-to-all-start.2 = ((bf16[256,16,1,128]{3,0,2,1:T(8,128)(2,1)}), bf16[256,16,1,128]{3,0,2,1:T(8,128)(2,1)S(1)}, u32[]{:S(2)}, u32[]{:S(2)}) async-start(bf16[256,16,1,128]{3,0,2,1:T(8,128)(2,1)} %copy.55), calls=%async_computation.2 | async-start | bytes 2097152 | tf_op jit(solution)/shard_map/all_to_all | solution.py:83
  58.8 65.0 %copy-start.6 = (s32[1,16,16]{2,1,0:T(8,128)S(1)}, s32[1,16,16]{2,1,0:T(8,128)}, u32[]{:S(2)}) copy-start(s32[1,16,16]{2,1,0:T(8,128)} %param.15) | copy-start | bytes 3076
  70.6 38.8 %all-to-all-start.6 = ((bf16[128,16,352]{0,2,1:T(8,128)(2,1)}), bf16[128,16,352]{0,2,1:T(8,128)(2,1)}, u32[]{:S(2)}, u32[]{:S(2)}) async-start(bf16[128,16,352]{0,2,1:T(8,128)(2,1)} %fusion.23), calls=%async_computation.6 | async-start | bytes 2883584 | tf_op jit(solution)/shard_map/all_to_all | solution.py:103
  109.4 53.5 %all-to-all-start.1 = ((bf16[256,16,1,128]{3,0,2,1:T(8,128)(2,1)}), bf16[256,16,1,128]{3,0,2,1:T(8,128)(2,1)S(1)}, u32[]{:S(2)}, u32[]{:S(2)}) async-start(bf16[256,16,1,128]{3,0,2,1:T(8,128)(2,1)} %copy.53), calls=%async_computation.1 | async-start | bytes 2097152 | tf_op jit(solution)/shard_map/all_to_all | solution.py:82
  123.7 156.3 %reduce-scatter.4.cloned.1.call-start = ((), (), s32[]{:S(2)}) async-start(), calls=%async_computation.8 | async-start | bytes 3604480 | tf_op jit(solution)/shard_map/reduce_scatter | solution.py:16
  124.9 38.1 %copy-start.5 = (s32[1,16]{1,0:T(1,128)S(1)}, s32[1,16]{1,0:T(1,128)}, u32[]{:S(2)}) copy-start(s32[1,16]{1,0:T(1,128)} %param.14) | copy-start | bytes 196
  163.2 2.1 copy-start.1
  163.2 2.1 copy-start.3
  175.3 4.9 %copy-start.2 = (bf16[4096,128]{1,0:T(8,128)(2,1)S(1)}, bf16[4096,128]{1,0:T(8,128)(2,1)}, u32[]{:S(2)}) copy-start(bf16[4096,128]{1,0:T(8,128)(2,1)} %copy-done.1) | copy-start | bytes 3145732 | tf_op jit(solution)/shard_map/while/body/eval_jaxpr/while
  180.2 6.2 %copy-start.4 = (bf16[2048,128]{1,0:T(8,128)(2,1)S(1)}, bf16[2048,128]{1,0:T(8,128)(2,1)}, u32[]{:S(2)}) copy-start(bf16[2048,128]{1,0:T(8,128)(2,1)} %copy-done.3) | copy-start | bytes 1572868 | tf_op jit(solution)/shard_map/while/body/eval_jaxpr/while
  186.4 2.0 copy-start.1
  186.4 2.0 copy-start.3
  198.5 4.9 %copy-start.2 = (bf16[4096,128]{1,0:T(8,128)(2,1)S(1)}, bf16[4096,128]{1,0:T(8,128)(2,1)}, u32[]{:S(2)}) copy-start(bf16[4096,128]{1,0:T(8,128)(2,1)} %copy-done.1) | copy-start | bytes 3145732 | tf_op jit(solution)/shard_map/while/body/eval_jaxpr/while
  203.4 6.2 %copy-start.4 = (bf16[2048,128]{1,0:T(8,128)(2,1)S(1)}, bf16[2048,128]{1,0:T(8,128)(2,1)}, u32[]{:S(2)}) copy-start(bf16[2048,128]{1,0:T(8,128)(2,1)} %copy-done.3) | copy-start | bytes 1572868 | tf_op jit(solution)/shard_map/while/body/eval_jaxpr/while
  209.5 2.0 copy-start.1
  209.5 2.0 copy-start.3
  221.7 4.8 %copy-start.2 = (bf16[4096,128]{1,0:T(8,128)(2,1)S(1)}, bf16[4096,128]{1,0:T(8,128)(2,1)}, u32[]{:S(2)}) copy-start(bf16[4096,128]{1,0:T(8,128)(2,1)} %copy-done.1) | copy-start | bytes 3145732 | tf_op jit(solution)/shard_map/while/body/eval_jaxpr/while
  226.5 6.2 %copy-start.4 = (bf16[2048,128]{1,0:T(8,128)(2,1)S(1)}, bf16[2048,128]{1,0:T(8,128)(2,1)}, u32[]{:S(2)}) copy-start(bf16[2048,128]{1,0:T(8,128)(2,1)} %copy-done.3) | copy-start | bytes 1572868 | tf_op jit(solution)/shard_map/while/body/eval_jaxpr/while
  232.7 2.0 copy-start.1
  232.7 2.0 copy-start.3
  244.8 4.8 %copy-start.2 = (bf16[4096,128]{1,0:T(8,128)(2,1)S(1)}, bf16[4096,128]{1,0:T(8,128)(2,1)}, u32[]{:S(2)}) copy-start(bf16[4096,128]{1,0:T(8,128)(2,1)} %copy-done.1) | copy-start | bytes 3145732 | tf_op jit(solution)/shard_map/while/body/eval_jaxpr/while
  249.6 6.2 %copy-start.4 = (bf16[2048,128]{1,0:T(8,128)(2,1)S(1)}, bf16[2048,128]{1,0:T(8,128)(2,1)}, u32[]{:S(2)}) copy-start(bf16[2048,128]{1,0:T(8,128)(2,1)} %copy-done.3) | copy-start | bytes 1572868 | tf_op jit(solution)/shard_map/while/body/eval_jaxpr/while
  255.8 55.1 %copy-start.7 = (u32[256]{0:T(256)S(1)}, u32[256]{0:T(256)}, u32[]{:S(2)}) copy-start(u32[256]{0:T(256)} %constant.63) | copy-start | bytes 3076
  259.3 13.6 %all-to-all-start.4 = ((bf16[16,2,8192]{2,1,0:T(2,128)(2,1)}), bf16[16,2,8192]{2,1,0:T(2,128)(2,1)S(1)}, u32[]{:S(2)}, u32[]{:S(2)}) async-start(bf16[16,2,8192]{2,1,0:T(2,128)(2,1)} %reshape.67), calls=%async_computation.4 | async-start | bytes 1048576 | tf_op jit(solution)/shard_map/all_to_all | solution.py:93
  272.9 41.2 %all-to-all-start.5 = ((bf16[16,2,8192]{2,1,0:T(2,128)(2,1)}), bf16[16,2,8192]{2,1,0:T(2,128)(2,1)S(1)}, u32[]{:S(2)}, u32[]{:S(2)}) async-start(bf16[16,2,8192]{2,1,0:T(2,128)(2,1)} %reshape.69), calls=%async_computation.5 | async-start | bytes 1048576 | tf_op jit(solution)/shard_map/all_to_all | solution.py:94
  305.6 10.4 %collective-permute-start = (bf16[4096,6]{0,1:T(8,128)(2,1)S(1)}, bf16[4096,6]{0,1:T(8,128)(2,1)S(1)}, u32[]{:S(2)}, u32[]{:S(2)}) collective-permute-start(bf16[4096,6]{0,1:T(8,128)(2,1)S(1)} %slice), channel_id=1, source_target_pairs={{0,1},{1,2},{2,3},{4,5},{5,6},{6,7},{8,9},{9,10},{10,11},{12,13},{... | collective-permute-start | bytes 147464
Sparse Core Ops, SparseCore 0:
  9.8 139.5 all-gather.2
  163.1 40.1 reduce-scatter.3
where the time goes:
time: 325 us; the launch traced here: 324 us
  waiting for transfers between devices  78.7 us (24%)
  starting transfers between devices  68.8 us (21%)
  matrix products  62.7 us (19%)
  local copies, waits for them, and re-layouts  40.5 us (12%)
  other arithmetic  27.3 us (8%)
  blocking collectives  25.5 us (8%)
  between operations  14.9 us (5%)
  loops' own time  5.57 us (2%)
    unnamed x1, blocking collectives  25.5 us
    all_gather x1, waiting for transfers between devices, per_device(): lax.all_gather(tokens, 'grp', axis=0, tiled=True)  24.6 us
    all_to_all x1, waiting for transfers between devices, per_device(): lax.all_to_all(up_cot, 'grp', split_axis=1, concat_axis=0, tiled=True)  23.1 us
    dot_general x4, matrix products, head_pass(): jnp.dot(grad_scores, key_head, preferred_element_type=jnp.float32)  21.5 us
    unnamed x25, local copies, waits for them, and re-layouts  15.8 us
    dot_general x4, matrix products, head_pass(): jnp.dot(weights_bf, value_head, preferred_element_type=jnp.float32)  14.9 us
    all_to_all x1, starting transfers between devices, per_device(): lax.all_to_all(split_heads(mem_keys), 'grp', split_axis=1, concat_axis=0,...  14.3 us
    dot_general x1, matrix products, per_device(): lax.dot_general(lax.all_gather(tokens, 'grp', axis=0, tiled=True), slices...  13.4 us
  transfers between devices with their start and end apart: 10, of which 6 were waited for; matrix products, arithmetic and copies ran while one was open for 48% of the time, Pallas kernels for 0%

commit v1 on v0

--- a/solution.py
+++ b/solution.py
@@ -102,7 +102,9 @@
     contract = (((0,), (0,)), ((), ()))
     slices = lax.all_to_all(up_cot, "grp", split_axis=1, concat_axis=0, tiled=True)
     partial_value = lax.dot_general(
-        lax.all_gather(tokens, "grp", axis=0, tiled=True),
+        jnp.concatenate(
+            lax.all_to_all(jnp.stack([tokens] * lax.axis_size("grp")), "grp", 0, 0), axis=0
+        ),
         slices,
         contract,
         preferred_element_type=jnp.float32,

time: 325 us -> 542 us (1.67)
  waiting for transfers between devices: 78.7 us -> 277 us
  blocking collectives: 25.5 us -> 46.3 us
  starting transfers between devices: 68.8 us -> 54.8 us
  local copies, waits for them, and re-layouts: 40.5 us -> 48.9 us
    all_to_all x1, waiting for transfers between devices: 23.1 us -> 255 us  [per_device(): lax.all_to_all(jnp.stack([tokens] * lax.axis_size('grp')), 'grp', 0, 0)]
    all_gather x1 -> x0, waiting for transfers between devices: 24.6 us -> none  [per_device(): lax.all_gather(tokens, 'grp', axis=0, tiled=True)]
    all_to_all x0 -> x1, blocking collectives: none -> 24.1 us  [per_device(): lax.all_to_all(up_cot, 'grp', split_axis=1, concat_axis=0, tiled=True)]
    all_to_all x1, starting transfers between devices: 14.3 us -> 7.17 us  [per_device(): lax.all_to_all(split_heads(mem_keys), 'grp', split_axis=1, concat_axis=0,...]
    all_to_all x1, waiting for transfers between devices: 11.8 us -> 4.89 us  [per_device(): lax.all_to_all(split_heads(mem_values), 'grp', split_axis=1, concat_axis=...]
    another operation x0 -> x1, local copies, waits for them, and re-layouts: none -> 6.85 us  [per_device(): jnp.stack([tokens] * lax.axis_size('grp'))]
    unnamed x25 -> x23, local copies, waits for them, and re-layouts: 15.8 us -> 12.3 us
  transfers between devices with their start and end apart: 10 -> 9, of which waited for: 6 -> 7; matrix products, arithmetic and copies ran while one was open for 48% -> 28% of each run, Pallas kernels for 0% -> 0%
where the time goes in v1:
time: 542 us; the launch traced here: 537 us
  waiting for transfers between devices  277 us (51%)
  matrix products  61.9 us (11%)
  starting transfers between devices  54.8 us (10%)
  local copies, waits for them, and re-layouts  48.9 us (9%)
  blocking collectives  46.3 us (9%)
  other arithmetic  27.3 us (5%)
  between operations  14.9 us (3%)
  loops' own time  5.9 us (1%)
    all_to_all x1, waiting for transfers between devices, per_device(): lax.all_to_all(jnp.stack([tokens] * lax.axis_size('grp')), 'grp', 0, 0)  255 us
    all_to_all x1, blocking collectives, per_device(): lax.all_to_all(up_cot, 'grp', split_axis=1, concat_axis=0, tiled=True)  24.1 us
    dot_general x4, matrix products, head_pass(): jnp.dot(grad_scores, key_head, preferred_element_type=jnp.float32)  22.7 us
    unnamed x1, blocking collectives  22.2 us
    dot_general x4, matrix products, head_pass(): jnp.dot(weights_bf, value_head, preferred_element_type=jnp.float32)  14.9 us
    convert_element_type x4, other arithmetic, head_pass(): weights_bf = (weights / row_total).astype(jnp.bfloat16)  13.2 us
    dot_general x4, matrix products, head_pass(): jnp.dot(query_head, key_head.T, preferred_element_type=jnp.float32)  13 us
    unnamed x23, local copies, waits for them, and re-layouts  12.3 us
  transfers between devices with their start and end apart: 9, of which 7 were waited for; matrix products, arithmetic and copies ran while one was open for 28% of the time, Pallas kernels for 0%

profile of v1, /device:TPU:72, one launch (start us, length us, event | category | flops | bytes accessed | tf_op | source)
XLA Modules:
  0.0 537.1 jit_solution(18165489732335269852)
XLA Ops:
  9.2 6.3 %all-to-all-start.3 = ((bf16[128,16,1,128]{0,3,2,1:T(8,128)(2,1)}), bf16[128,16,1,128]{0,3,2,1:T(8,128)(2,1)S(1)}, u32[]{:S(2)}, u32[]{:S(2)}) async-start(bf16[128,16,1,128]{0,3,2,1:T(8,128)(2,1)} %bitcast.13), calls=%async_computation.3 | async-start | bytes 1048576 | tf_op jit(solution)/shard_map/all_to_all | solution.py:84
  17.8 4.9 all-to-all-done.3
  22.7 7.1 %all-to-all-start = ((bf16[128,16,1,128]{3,0,2,1:T(8,128)(2,1)}), bf16[128,16,1,128]{3,0,2,1:T(8,128)(2,1)S(1)}, u32[]{:S(2)}, u32[]{:S(2)}) async-start(bf16[128,16,1,128]{3,0,2,1:T(8,128)(2,1)} %copy.50), calls=%async_computation | async-start | bytes 1048576 | tf_op jit(solution)/shard_map/all_to_all | solution.py:81
  32.6 4.5 all-to-all-done
  37.1 7.1 %all-to-all-start.2 = ((bf16[256,16,1,128]{3,0,2,1:T(8,128)(2,1)}), bf16[256,16,1,128]{3,0,2,1:T(8,128)(2,1)S(1)}, u32[]{:S(2)}, u32[]{:S(2)}) async-start(bf16[256,16,1,128]{3,0,2,1:T(8,128)(2,1)} %copy.54), calls=%async_computation.2 | async-start | bytes 2097152 | tf_op jit(solution)/shard_map/all_to_all | solution.py:83
  49.2 3.4 multiply_convert_fusion.1
  52.7 4.9 all-to-all-done.2
  57.6 24.1 %all_to_all.108 = bf16[128,16,352]{0,2,1:T(8,128)(2,1)} all-to-all(bf16[128,16,352]{0,2,1:T(8,128)(2,1)S(1)} %multiply_convert_fusion.1), channel_id=1, replica_groups=mesh['grp'=16,'dp_0'=4,'dp_1'=4] {'grp'}, dimensions={1} | all-to-all | bytes 2883584 | tf_op jit(solution)/shard_map/all_to_all | solution.py:103
  81.7 6.9 %stack.3 = bf16[16,128,4096]{2,1,0:T(8,128)(2,1)} broadcast(bf16[128,4096]{1,0:T(8,128)(2,1)} %bitcast.109), dimensions={1,2} | broadcast | bytes 17825792 | tf_op jit(solution)/shard_map/stack | solution.py:106
  88.5 8.1 %all-to-all-start.7 = ((bf16[16,128,4096]{2,1,0:T(8,128)(2,1)}), bf16[16,128,4096]{2,1,0:T(8,128)(2,1)}, u32[]{:S(2)}, u32[]{:S(2)}) async-start(bf16[16,128,4096]{2,1,0:T(8,128)(2,1)} %stack.3), calls=%async_computation.7 | async-start | bytes 33554432 | tf_op jit(solution)/shard_map/all_to_all | solution.py:106
  100.5 255.4 %all-to-all-done.7 = bf16[16,128,4096]{2,1,0:T(8,128)(2,1)} async-done(((bf16[16,128,4096]{2,1,0:T(8,128)(2,1)}), bf16[16,128,4096]{2,1,0:T(8,128)(2,1)}, u32[]{:S(2)}, u32[]{:S(2)}) %all-to-all-start.7) | async-done | bytes 16777248 | tf_op jit(solution)/shard_map/all_to_all | solution.py:106
  356.0 7.2 %all-to-all-start.1 = ((bf16[256,16,1,128]{3,0,2,1:T(8,128)(2,1)}), bf16[256,16,1,128]{3,0,2,1:T(8,128)(2,1)}, u32[]{:S(2)}, u32[]{:S(2)}) async-start(bf16[256,16,1,128]{3,0,2,1:T(8,128)(2,1)} %copy.52), calls=%async_computation.1 | async-start | bytes 2097152 | tf_op jit(solution)/shard_map/all_to_all | solution.py:82
  363.2 11.3 %fusion.12 = bf16[4096,352]{0,1:T(8,128)(2,1)} fusion(bf16[16,128,4096]{2,1,0:T(8,128)(2,1)} %all-to-all-done.7, bf16[128,16,352]{0,2,1:T(8,128)(2,1)} %all_to_all.108), kind=kOutput, calls=%fused_computation.22 | convolution fusion | flops 5907021824 | bytes 21102592 | tf_op jit(solution)/shard_map/dot_general | solution.py:104
  376.6 94.4 %while.22 = (s32[]{:T(128)}, bf16[4,512,128]{2,1,0:T(8,128)(2,1)}, bf16[4,512,128]{2,1,0:T(8,128)(2,1)}, s32[4]{0:T(128)S(1)}, pred[16,16]{1,0:T(8,128)(4,1)S(1)...) while((s32[]{:T(128)}, bf16[4,512,128]{2,1,0:T(8,128)(2,1)}, ...), condition=%wide.region_4.5_spmd.clone, body=%wide.region_0.4_spmd.clone.sunk | while | flops 2173127168 | bytes 56286784 | solution.py:74
  385.7 3.3 divide_convert_fusion.2
  390.0 3.7 multiply_reduce_fusion.2
  393.8 5.7 %fusion.40 = bf16[4,512,128]{2,1,0:T(8,128)(2,1)} fusion(bf16[4,512,128]{2,1,0:T(8,128)(2,1)} %get-tuple-element.278, s32[]{:T(128)} %get-tuple-element.276, bf16[4096,128]{1,0:T(8,128)(2,1)} %get-tuple-element.298, bf16[512,4096]{1,0:T(8,128)(2,1)} %divide_convert_fusion.2, bf16[512,128]{1,0:T(8,128)(2,1)S(1)} %constant_dynamic-slice_fusion.4, ...), kind=kOutput, calls=%fused_computation.11.clone.1 | convolution fusion | flops 1082261504 | bytes 6556160 | tf_op jit(solution)/shard_map/while/body/eval_jaxpr/while/body/eval_jaxpr/dot_general | solution.py:37
  404.8 3.3 fusion.38
  409.3 3.3 divide_convert_fusion.2
  413.7 3.8 multiply_reduce_fusion.2
  417.5 5.7 %fusion.40 = bf16[4,512,128]{2,1,0:T(8,128)(2,1)} fusion(bf16[4,512,128]{2,1,0:T(8,128)(2,1)} %get-tuple-element.278, s32[]{:T(128)} %get-tuple-element.276, bf16[4096,128]{1,0:T(8,128)(2,1)} %get-tuple-element.298, bf16[512,4096]{1,0:T(8,128)(2,1)} %divide_convert_fusion.2, bf16[512,128]{1,0:T(8,128)(2,1)S(1)} %constant_dynamic-slice_fusion.4, ...), kind=kOutput, calls=%fused_computation.11.clone.1 | convolution fusion | flops 1082261504 | bytes 6556160 | tf_op jit(solution)/shard_map/while/body/eval_jaxpr/while/body/eval_jaxpr/dot_general | solution.py:37
  433.0 3.3 divide_convert_fusion.2
  437.3 3.7 multiply_reduce_fusion.2
  441.0 5.7 %fusion.40 = bf16[4,512,128]{2,1,0:T(8,128)(2,1)} fusion(bf16[4,512,128]{2,1,0:T(8,128)(2,1)} %get-tuple-element.278, s32[]{:T(128)} %get-tuple-element.276, bf16[4096,128]{1,0:T(8,128)(2,1)} %get-tuple-element.298, bf16[512,4096]{1,0:T(8,128)(2,1)} %divide_convert_fusion.2, bf16[512,128]{1,0:T(8,128)(2,1)S(1)} %constant_dynamic-slice_fusion.4, ...), kind=kOutput, calls=%fused_computation.11.clone.1 | convolution fusion | flops 1082261504 | bytes 6556160 | tf_op jit(solution)/shard_map/while/body/eval_jaxpr/while/body/eval_jaxpr/dot_general | solution.py:37
  456.5 3.3 divide_convert_fusion.2
  460.8 3.7 multiply_reduce_fusion.2
  464.6 5.7 %fusion.40 = bf16[4,512,128]{2,1,0:T(8,128)(2,1)} fusion(bf16[4,512,128]{2,1,0:T(8,128)(2,1)} %get-tuple-element.278, s32[]{:T(128)} %get-tuple-element.276, bf16[4096,128]{1,0:T(8,128)(2,1)} %get-tuple-element.298, bf16[512,4096]{1,0:T(8,128)(2,1)} %divide_convert_fusion.2, bf16[512,128]{1,0:T(8,128)(2,1)S(1)} %constant_dynamic-slice_fusion.4, ...), kind=kOutput, calls=%fused_computation.11.clone.1 | convolution fusion | flops 1082261504 | bytes 6556160 | tf_op jit(solution)/shard_map/while/body/eval_jaxpr/while/body/eval_jaxpr/dot_general | solution.py:37
  474.5 6.6 %all-to-all-start.4 = ((bf16[16,2,8192]{2,1,0:T(2,128)(2,1)}), bf16[16,2,8192]{2,1,0:T(2,128)(2,1)S(1)}, u32[]{:S(2)}, u32[]{:S(2)}) async-start(bf16[16,2,8192]{2,1,0:T(2,128)(2,1)} %reshape.70), calls=%async_computation.4 | async-start | bytes 1048576 | tf_op jit(solution)/shard_map/all_to_all | solution.py:93
  484.1 4.3 all-to-all-done.4
  488.5 7.1 %all-to-all-start.5 = ((bf16[16,2,8192]{2,1,0:T(2,128)(2,1)}), bf16[16,2,8192]{2,1,0:T(2,128)(2,1)S(1)}, u32[]{:S(2)}, u32[]{:S(2)}) async-start(bf16[16,2,8192]{2,1,0:T(2,128)(2,1)} %reshape.72), calls=%async_computation.5 | async-start | bytes 1048576 | tf_op jit(solution)/shard_map/all_to_all | solution.py:94
  495.5 22.2 %fusion.2 = bf16[4096,24]{0,1:T(8,128)(2,1)S(1)} fusion(bf16[4096,88]{0,1:T(8,128)(2,1)} %reduce-scatter.4.cloned.1.call-done), kind=kCustom, calls=%all-reduce-scatter | all-reduce-scatter fusion | flops 393217 | bytes 918528
  517.8 5.3 collective-permute-start
  (108 shorter events, 65.6 us)
Async XLA Ops:
  9.2 13.5 %all-to-all-start.3 = ((bf16[128,16,1,128]{0,3,2,1:T(8,128)(2,1)}), bf16[128,16,1,128]{0,3,2,1:T(8,128)(2,1)S(1)}, u32[]{:S(2)}, u32[]{:S(2)}) async-start(bf16[128,16,1,128]{0,3,2,1:T(8,128)(2,1)} %bitcast.13), calls=%async_computation.3 | async-start | bytes 1048576 | tf_op jit(solution)/shard_map/all_to_all | solution.py:84
  16.8 27.4 %copy-start = (bf16[1,1,128,5632]{3,2,1,0:T(8,128)(2,1)S(1)}, bf16[1,1,128,5632]{3,2,1,0:T(8,128)(2,1)}, u32[]{:S(2)}) copy-start(bf16[1,1,128,5632]{3,2,1,0:T(8,128)(2,1)} %param.19) | copy-start | bytes 4325380
  22.7 14.4 %all-to-all-start = ((bf16[128,16,1,128]{3,0,2,1:T(8,128)(2,1)}), bf16[128,16,1,128]{3,0,2,1:T(8,128)(2,1)S(1)}, u32[]{:S(2)}, u32[]{:S(2)}) async-start(bf16[128,16,1,128]{3,0,2,1:T(8,128)(2,1)} %copy.50), calls=%async_computation | async-start | bytes 1048576 | tf_op jit(solution)/shard_map/all_to_all | solution.py:81
  37.1 20.5 %all-to-all-start.2 = ((bf16[256,16,1,128]{3,0,2,1:T(8,128)(2,1)}), bf16[256,16,1,128]{3,0,2,1:T(8,128)(2,1)S(1)}, u32[]{:S(2)}, u32[]{:S(2)}) async-start(bf16[256,16,1,128]{3,0,2,1:T(8,128)(2,1)} %copy.54), calls=%async_computation.2 | async-start | bytes 2097152 | tf_op jit(solution)/shard_map/all_to_all | solution.py:83
  88.5 267.4 %all-to-all-start.7 = ((bf16[16,128,4096]{2,1,0:T(8,128)(2,1)}), bf16[16,128,4096]{2,1,0:T(8,128)(2,1)}, u32[]{:S(2)}, u32[]{:S(2)}) async-start(bf16[16,128,4096]{2,1,0:T(8,128)(2,1)} %stack.3), calls=%async_computation.7 | async-start | bytes 33554432 | tf_op jit(solution)/shard_map/all_to_all | solution.py:106
  96.6 2.9 copy-start.4
  356.0 20.7 %all-to-all-start.1 = ((bf16[256,16,1,128]{3,0,2,1:T(8,128)(2,1)}), bf16[256,16,1,128]{3,0,2,1:T(8,128)(2,1)}, u32[]{:S(2)}, u32[]{:S(2)}) async-start(bf16[256,16,1,128]{3,0,2,1:T(8,128)(2,1)} %copy.52), calls=%async_computation.1 | async-start | bytes 2097152 | tf_op jit(solution)/shard_map/all_to_all | solution.py:82
  363.1 13.5 %copy-start.3 = (s32[1,16]{1,0:T(1,128)S(1)}, s32[1,16]{1,0:T(1,128)}, u32[]{:S(2)}) copy-start(s32[1,16]{1,0:T(1,128)} %param.14) | copy-start | bytes 196
  363.1 132.4 %reduce-scatter.4.cloned.1.call-start = ((), (), s32[]{:S(2)}) async-start(), calls=%async_computation.9 | async-start | bytes 3604480 | tf_op jit(solution)/shard_map/reduce_scatter | solution.py:16
  376.6 2.2 copy-start.1
  393.8 6.5 %copy-start.2 = (bf16[2048,128]{1,0:T(8,128)(2,1)S(1)}, bf16[2048,128]{1,0:T(8,128)(2,1)}, u32[]{:S(2)}) copy-start(bf16[2048,128]{1,0:T(8,128)(2,1)} %copy-done.1) | copy-start | bytes 1572868 | tf_op jit(solution)/shard_map/while/body/eval_jaxpr/while
  400.3 2.2 copy-start.1
  417.5 6.5 %copy-start.2 = (bf16[2048,128]{1,0:T(8,128)(2,1)S(1)}, bf16[2048,128]{1,0:T(8,128)(2,1)}, u32[]{:S(2)}) copy-start(bf16[2048,128]{1,0:T(8,128)(2,1)} %copy-done.1) | copy-start | bytes 1572868 | tf_op jit(solution)/shard_map/while/body/eval_jaxpr/while
  423.9 2.2 copy-start.1
  441.0 6.5 %copy-start.2 = (bf16[2048,128]{1,0:T(8,128)(2,1)S(1)}, bf16[2048,128]{1,0:T(8,128)(2,1)}, u32[]{:S(2)}) copy-start(bf16[2048,128]{1,0:T(8,128)(2,1)} %copy-done.1) | copy-start | bytes 1572868 | tf_op jit(solution)/shard_map/while/body/eval_jaxpr/while
  447.5 2.2 copy-start.1
  464.6 6.5 %copy-start.2 = (bf16[2048,128]{1,0:T(8,128)(2,1)S(1)}, bf16[2048,128]{1,0:T(8,128)(2,1)}, u32[]{:S(2)}) copy-start(bf16[2048,128]{1,0:T(8,128)(2,1)} %copy-done.1) | copy-start | bytes 1572868 | tf_op jit(solution)/shard_map/while/body/eval_jaxpr/while
  471.0 52.0 %copy-start.5 = (u32[256]{0:T(256)S(1)}, u32[256]{0:T(256)}, u32[]{:S(2)}) copy-start(u32[256]{0:T(256)} %constant.63) | copy-start | bytes 3076
  474.5 13.9 %all-to-all-start.4 = ((bf16[16,2,8192]{2,1,0:T(2,128)(2,1)}), bf16[16,2,8192]{2,1,0:T(2,128)(2,1)S(1)}, u32[]{:S(2)}, u32[]{:S(2)}) async-start(bf16[16,2,8192]{2,1,0:T(2,128)(2,1)} %reshape.70), calls=%async_computation.4 | async-start | bytes 1048576 | tf_op jit(solution)/shard_map/all_to_all | solution.py:93
  488.5 37.8 %all-to-all-start.5 = ((bf16[16,2,8192]{2,1,0:T(2,128)(2,1)}), bf16[16,2,8192]{2,1,0:T(2,128)(2,1)S(1)}, u32[]{:S(2)}, u32[]{:S(2)}) async-start(bf16[16,2,8192]{2,1,0:T(2,128)(2,1)} %reshape.72), calls=%async_computation.5 | async-start | bytes 1048576 | tf_op jit(solution)/shard_map/all_to_all | solution.py:94
  517.8 11.3 %collective-permute-start = (bf16[4096,6]{0,1:T(8,128)(2,1)S(1)}, bf16[4096,6]{0,1:T(8,128)(2,1)S(1)}, u32[]{:S(2)}, u32[]{:S(2)}) collective-permute-start(bf16[4096,6]{0,1:T(8,128)(2,1)S(1)} %slice), channel_id=1, source_target_pairs={{0,1},{1,2},{2,3},{4,5},{5,6},{6,7},{8,9},{9,10},{10,11},{12,13},{... | collective-permute-start | bytes 147464
Sparse Core Ops, SparseCore 0:
  374.6 39.7 reduce-scatter.3
